TPU v7x, 32 devices: a whole 2x2x4 slice. The times are simulated.
32 devices in a mesh: dp: 2 (over x), fsdp: 4 (over z), expert: 4 (over y, core).
Axes of the slice: x: 2, y: 2, z: 4, core: 2. Of those that a mesh axis runs over, the one named last changes fastest.
Arguments:
- window: bfloat16 [256, 4096], P('fsdp'), may hold values from -3 to 3
- attention_gain: float32 [4096], replicated, may hold values from 0.1 to 1.9
- query_weight: bfloat16 [4096, 4096], P('fsdp', 'expert'), may hold values from -0.09375 to 0.09375
- key_weight: bfloat16 [4096, 1024], P('fsdp', 'expert'), may hold values from -0.1875 to 0.1875
- value_weight: bfloat16 [4096, 1024], P('fsdp', 'expert'), may hold values from -0.1875 to 0.1875
- out_weight: bfloat16 [4096, 4096], P('expert', 'fsdp'), may hold values from -0.1875 to 0.1875
- cache_keys: bfloat16 [1024, 1024], P('dp', 'expert'), may hold values from -104 to 104
- cache_values: bfloat16 [1024, 1024], P('dp', 'expert'), may hold values from -12 to 12
- occluded: int32 [1024, 2], P('dp'), may hold values from 0 to 1, as said below
- feedforward_gain: float32 [4096], replicated, may hold values from 0.1 to 1.9
- router_weight: bfloat16 [4096, 4], replicated, may hold values from -0.0234375 to 0.0234375
- chosen_experts: int32 [2, 256, 2], P('dp', 'fsdp'), may hold values from 0 to 3, all different within a row; in each aligned block of 64 rows (0 to 63, 64 to 127, ..., all dimensions but the last counted through in order) at most 64 rows name the same one
- gate_weight: bfloat16 [4, 12288, 4096], P('expert', ('dp', 'fsdp')), may hold values from -0.09375 to 0.09375
- up_weight: bfloat16 [4, 12288, 4096], P('expert', ('dp', 'fsdp')), may hold values from -0.09375 to 0.09375
- down_weight: bfloat16 [4, 12288, 4096], P('expert', ('dp', 'fsdp')), may hold values from -0.0546875 to 0.0546875
Outputs:
- layer_output: bfloat16 [2, 256, 4096], P('dp', 'fsdp')
Inputs may be any that keep to these rules, and one draw needn't show every extreme that they name: `chosen_experts`: each row names 2 different experts. In each aligned block of 64 rows, counting the leading dimensions together (the rows of one device), no expert is named by more than 64 rows, a bound that some block reaches. `occluded`: constant over each aligned run of 64 prefix positions.
All inputs are finite; a program needn't handle non-finite values.
Results may differ from a plain program's by a relative error of at most 0.0095.
The roundings to bfloat16 on the way count: a program that leaves them out, or rounds other values in their place, can miss the bound.
Values may be sent and summed in bfloat16 or wider, within the bound.
A program may use at most 128 MiB of HBM per device.

v0:
```python
import jax
import jax.numpy as jnp
from jax import lax
from jax.sharding import PartitionSpec as P

HD = 128
TOP = 2
epsilon = 1e-05
rope_base = 1000000.0
floor_score = -1e30


def rms_norm(values, scales):
    widened = values.astype(jnp.float32)
    inverse = lax.rsqrt(jnp.mean(widened * widened, axis=-1, keepdims=True) + epsilon)
    return (widened * inverse * scales).astype(jnp.bfloat16)


def rotate(vectors, positions):
    halfway = vectors.shape[-1] // 2
    powers = jnp.arange(halfway, dtype=jnp.float32) * (2.0 / vectors.shape[-1])
    frequency = rope_base ** (-powers)
    angles = positions.astype(jnp.float32)[:, None] * frequency[None, :]
    cosine = jnp.cos(angles)[:, None, :]
    sine_part = jnp.sin(angles)[:, None, :]
    former = vectors[..., :halfway]
    latter = vectors[..., halfway:]
    return jnp.concatenate(
        [former * cosine - latter * sine_part, latter * cosine + former * sine_part], axis=-1
    )


def absorb_block(running, scores, visible, values_block):
    running_top, running_total, running_output = running
    masked = jnp.where(visible, scores, floor_score)
    fresh_top = jnp.maximum(running_top, jnp.max(masked, axis=-1))
    weights = jnp.where(visible, jnp.exp(masked - fresh_top[..., None]), 0.0)
    fresh_total = jnp.sum(weights, axis=-1)
    fresh_output = jnp.einsum(
        "kgtn,nkd->kgtd",
        weights.astype(jnp.bfloat16),
        values_block,
        preferred_element_type=jnp.float32,
    )
    return (fresh_top, fresh_total, fresh_output)


def local(
    window,
    attention_gain,
    query_weight,
    key_weight,
    value_weight,
    out_weight,
    cache_keys,
    cache_values,
    occluded,
    feedforward_gain,
    router_weight,
    chosen_experts,
    gate_weight,
    up_weight,
    down_weight,
):
    token_rows = window.shape[0]
    fsdp_count = lax.axis_size("fsdp")
    fsdp_place = lax.axis_index("fsdp")
    data_place = lax.axis_index("dp")
    expert_place = lax.axis_index("expert")
    query_heads = query_weight.shape[1] // HD
    key_heads = key_weight.shape[1] // HD
    grouping = query_heads // key_heads
    window_rows = token_rows * fsdp_count
    prefix_rows = cache_keys.shape[0] * lax.axis_size("dp")
    score_scale = HD ** (-0.5)
    normed = rms_norm(window, attention_gain)
    first_row = fsdp_place * token_rows
    own_positions = prefix_rows + first_row + jnp.arange(token_rows, dtype=jnp.int32)
    all_positions = prefix_rows + jnp.arange(window_rows, dtype=jnp.int32)
    everyone = lax.all_gather(normed, "fsdp", axis=0, tiled=True)
    slab_width = query_weight.shape[0]
    columns = lax.dynamic_slice_in_dim(everyone, fsdp_place * slab_width, slab_width, 1)
    row_block = columns
    query_sum = lax.psum_scatter(
        jnp.dot(row_block, query_weight, preferred_element_type=jnp.float32),
        "fsdp",
        scatter_dimension=0,
        tiled=True,
    )
    key_sum, value_sum = lax.psum(
        (
            jnp.dot(columns, key_weight, preferred_element_type=jnp.float32),
            jnp.dot(columns, value_weight, preferred_element_type=jnp.float32),
        ),
        "fsdp",
    )
    queries = rotate(query_sum.reshape(token_rows, query_heads, HD), own_positions).astype(
        jnp.bfloat16
    )
    window_keys = (
        rotate(key_sum.reshape(window_rows, key_heads, HD), all_positions)
        .astype(jnp.bfloat16)
        .reshape(window_rows, key_heads * HD)
    )
    window_values = value_sum.astype(jnp.bfloat16)
    query_grid = queries.reshape(token_rows, key_heads, grouping, HD)
    fresh_keys = window_keys.reshape(window_rows, key_heads, HD)
    fresh_values = window_values.reshape(window_rows, key_heads, HD)
    window_scores = (
        jnp.einsum("tkgd,nkd->kgtn", query_grid, fresh_keys, preferred_element_type=jnp.float32)
        * score_scale
    )
    causal = jnp.arange(window_rows)[None, :] <= (first_row + jnp.arange(token_rows))[:, None]
    empty_state = (
        jnp.full((key_heads, grouping, token_rows), floor_score, jnp.float32),
        jnp.zeros((key_heads, grouping, token_rows), jnp.float32),
        jnp.zeros((key_heads, grouping, token_rows, HD), jnp.float32),
    )
    window_state = absorb_block(empty_state, window_scores, causal, fresh_values)
    occluded_flags = occluded.astype(jnp.bfloat16)
    keys_block = lax.all_gather(cache_keys, "dp", axis=0, tiled=True)
    values_block = lax.all_gather(cache_values, "dp", axis=0, tiled=True)
    flags_block = lax.all_gather(occluded_flags, "dp", axis=0, tiled=True)
    block_length = keys_block.shape[0]
    scores = (
        jnp.einsum(
            "tkgd,nkd->kgtn",
            query_grid,
            keys_block.reshape(block_length, key_heads, HD),
            preferred_element_type=jnp.float32,
        )
        * score_scale
    )
    visible = lax.dynamic_slice_in_dim(flags_block, data_place, 1, 1)[:, 0] == 0
    prefix_state = absorb_block(
        empty_state, scores, visible, values_block.reshape(block_length, key_heads, HD)
    )
    overall = jnp.maximum(prefix_state[0], window_state[0])
    prefix_fade = jnp.exp(prefix_state[0] - overall)
    window_fade = jnp.exp(window_state[0] - overall)
    denominator = prefix_state[1] * prefix_fade + window_state[1] * window_fade
    head_values = (
        prefix_state[2] * prefix_fade[..., None] + window_state[2] * window_fade[..., None]
    ) / denominator[..., None]
    attended = (
        head_values.transpose(2, 0, 1, 3).reshape(token_rows, query_heads * HD).astype(jnp.bfloat16)
    )
    head_terms = jnp.dot(
        attended,
        lax.all_gather(out_weight, "fsdp", axis=1, tiled=True),
        preferred_element_type=jnp.float32,
    )
    residual = window.astype(jnp.float32) + lax.psum(head_terms, "expert")
    normed_mix = rms_norm(residual, feedforward_gain)
    logits = jnp.dot(normed_mix, router_weight, preferred_element_type=jnp.float32)
    expert_count = router_weight.shape[1]
    expert_picks = chosen_experts.reshape(token_rows, TOP)
    matches = expert_picks[:, :, None] == jnp.arange(expert_count, dtype=jnp.int32)[None, None, :]
    picked = jnp.sum(jnp.where(matches, logits[:, None, :], 0.0), axis=-1)
    gate_shares = jax.nn.sigmoid(picked - picked[:, ::-1])
    expert_hits = expert_picks == expert_place
    taken_flag = jnp.any(expert_hits, axis=1).astype(jnp.int32)
    weight_mine = jnp.sum(jnp.where(expert_hits, gate_shares, 0.0), axis=1)
    capacity = min(token_rows, 2 * token_rows * TOP // expert_count)
    slot_numbers = jnp.cumsum(taken_flag) - taken_flag
    placing = (slot_numbers[:, None] == jnp.arange(capacity, dtype=jnp.int32)[None, :]) & (
        taken_flag[:, None] == 1
    )
    send_rows = lax.dot_general(
        placing.astype(jnp.bfloat16),
        normed_mix,
        (((0,), (0,)), ((), ())),
        preferred_element_type=jnp.float32,
    ).astype(jnp.bfloat16)
    gate_rows = gate_weight[0]
    up_rows = up_weight[0]
    down_rows = down_weight[0]
    contract_last = (((1,), (1,)), ((), ()))
    piece_rows = lax.all_gather(send_rows, ("dp", "fsdp"), axis=0, tiled=True)
    gate_values = lax.dot_general(
        piece_rows, gate_rows, contract_last, preferred_element_type=jnp.float32
    )
    lifted = lax.dot_general(piece_rows, up_rows, contract_last, preferred_element_type=jnp.float32)
    hidden = (jax.nn.silu(gate_values) * lifted).astype(jnp.bfloat16)
    row_block = hidden
    expert_output = lax.psum_scatter(
        jnp.dot(row_block, down_rows, preferred_element_type=jnp.float32).astype(jnp.bfloat16),
        ("dp", "fsdp"),
        scatter_dimension=0,
        tiled=True,
    ).astype(jnp.float32)
    returned = jnp.dot(
        placing.astype(jnp.float32),
        expert_output,
        precision=lax.Precision.HIGHEST,
        preferred_element_type=jnp.float32,
    )
    mixture = lax.psum(returned * weight_mine[:, None], "expert")
    return (residual + mixture).astype(jnp.bfloat16).reshape(1, token_rows, residual.shape[1])


def solution(mesh):
    placed = (
        P("fsdp", None),
        P(),
        P("fsdp", "expert"),
        P("fsdp", "expert"),
        P("fsdp", "expert"),
        P("expert", "fsdp"),
        P("dp", "expert"),
        P("dp", "expert"),
        P("dp", None),
        P(),
        P(),
        P("dp", "fsdp", None),
        P("expert", ("dp", "fsdp"), None),
        P("expert", ("dp", "fsdp"), None),
        P("expert", ("dp", "fsdp"), None),
    )
    return jax.shard_map(
        local, mesh=mesh, in_specs=placed, out_specs=P("dp", "fsdp", None), check_vma=False
    )
```

profile of v0, /device:TPU:0, one launch (start us, length us, event | category | flops | bytes accessed | tf_op | source)
XLA Modules:
  0.0 560.7 jit_solution(14526967308801473713)
XLA Ops:
  6.5 1.4 fusion.29
  8.0 2.0 fusion.31
  10.1 48.7 %all-gather.4.cloned.1.call-done = bf16[256,4096]{1,0:T(8,128)(2,1)} async-done(((bf16[64,4096]{1,0:T(8,128)(2,1)}), bf16[256,4096]{1,0:T(8,128)(2,1)}) %all-gather.4.cloned.1.call-update) | async-done | bytes 2097168 | tf_op jit(solution)/shard_map/all_gather | solution.py:80
  58.8 1.4 fusion.43
  60.2 0.8 copy.41
  61.1 2.7 fusion.45
  63.9 0.5 all-gather.6.cloned.1.call-update
  65.1 4.3 all_gather.18
  69.5 7.9 %all_gather.20 = bf16[1024,256]{0,1:T(8,128)(2,1)S(1)} all-gather(bf16[512,256]{0,1:T(8,128)(2,1)S(1)} %copy.37), channel_id=1, replica_groups=mesh['dp'=2,'fsdp'=4,'expert'=4] {'dp'}, dimensions={0}, use_global_device_ids=true | all-gather | bytes 786432 | tf_op jit(solution)/shard_map/all_gather | solution.py:121
  77.4 7.1 %all_gather.21 = bf16[1024,256]{0,1:T(8,128)(2,1)S(1)} all-gather(bf16[512,256]{0,1:T(8,128)(2,1)S(1)} %copy.39), channel_id=1, replica_groups=mesh['dp'=2,'fsdp'=4,'expert'=4] {'dp'}, dimensions={0}, use_global_device_ids=true | all-gather | bytes 786432 | tf_op jit(solution)/shard_map/all_gather | solution.py:122
  84.8 0.5 multiply_cosine_fusion
  85.3 1.3 fusion.41
  86.7 23.1 %all-reduce.10 = bf16[256,256]{1,0:T(8,128)(2,1)S(1)} all-reduce(f32[256,256]{1,0:T(8,128)S(1)} %fusion.41), channel_id=1, replica_groups=mesh['dp'=2,'fsdp'=4,'expert'=4] {'fsdp'}, use_global_device_ids=true, to_apply=%region_5.6 | all-reduce | flops 65536 | bytes 393216 | tf_op jit(solution)/shard_map/psum | solution.py:90
  109.9 1.2 subtract_convert_fusion
  111.1 14.3 %reduce-scatter.3.cloned.1.call-done = f32[64,1024]{1,0:T(8,128)} async-done(((f32[256,1024]{1,0:T(8,128)}), f32[64,1024]{1,0:T(8,128)}) %reduce-scatter.3.cloned.1.call-update) | async-done | bytes 262160 | tf_op jit(solution)/shard_map/reduce_scatter | solution.py:84
  125.4 1.0 copy.55
  127.3 0.6 bitcast_reduce_fusion
  127.9 0.6 fusion.20
  128.6 0.6 fusion.27
  129.8 145.4 %all-gather.6.cloned.1.call-done = bf16[1024,4096]{1,0:T(8,128)(2,1)} async-done(((bf16[1024,1024]{1,0:T(8,128)(2,1)}), bf16[1024,4096]{1,0:T(8,128)(2,1)}) %all-gather.6.cloned.1.call-update) | async-done | bytes 8388624 | tf_op jit(solution)/shard_map/all_gather | solution.py:150
  275.1 6.0 %fusion.80 = f32[64,4096]{1,0:T(8,128)} fusion(bf16[64,1024]{1,0:T(8,128)(2,1)S(1)} %convert_element_type.96, bf16[1024,4096]{1,0:T(8,128)(2,1)} %all-gather.6.cloned.1.call-done), kind=kOutput, calls=%fused_computation.113 | convolution fusion | flops 536870912 | bytes 9568256 | tf_op jit(solution)/shard_map/dot_general | solution.py:148
  281.6 34.0 %all-reduce.7.cloned.1.call-done = f32[64,4096]{1,0:T(8,128)} async-done(((f32[64,4096]{1,0:T(8,128)}), f32[64,4096]{1,0:T(8,128)}) %all-reduce.7.cloned.1.call-update) | async-done | bytes 1048592 | tf_op jit(solution)/shard_map/psum | solution.py:153
  315.6 1.6 multiply_reduce_fusion
  317.4 1.2 convolution_convert_fusion
  318.9 73.7 %all-gather.8.cloned.1.call-done = bf16[512,4096]{1,0:T(8,128)(2,1)} async-done(((bf16[64,4096]{1,0:T(8,128)(2,1)}), bf16[512,4096]{1,0:T(8,128)(2,1)}) %all-gather.8.cloned.1.call-update) | async-done | bytes 4194320 | tf_op jit(solution)/shard_map/all_gather | solution.py:179
  392.6 12.1 %fusion.4 = f32[512,1536]{1,0:T(8,128)} fusion(bf16[512,4096]{1,0:T(8,128)(2,1)} %all-gather.8.cloned.1.call-done, bf16[1,1536,4096]{2,1,0:T(8,128)(2,1)} %param.27), kind=kOutput, calls=%fused_computation.4 | convolution fusion | flops 6442450944 | bytes 19922944 | tf_op jit(solution)/shard_map/dot_general | solution.py:180
  404.7 21.8 %fusion.6 = bf16[512,4096]{1,0:T(8,128)(2,1)} fusion(bf16[1,1536,4096]{2,1,0:T(8,128)(2,1)} %param.29, bf16[512,4096]{1,0:T(8,128)(2,1)} %all-gather.8.cloned.1.call-done, bf16[1,1536,4096]{2,1,0:T(8,128)(2,1)} %param.28, f32[512,1536]{1,0:T(8,128)} %fusion.4), kind=kOutput, calls=%fused_computation.6 | convolution fusion | flops 12891717632 | bytes 36700160 | tf_op jit(solution)/shard_map/dot_general | solution.py:187
  426.6 0.7 copy-done.8
  427.6 85.3 %reduce-scatter.5.cloned.1.call-done = bf16[64,4096]{1,0:T(8,128)(2,1)} async-done(((bf16[512,4096]{1,0:T(8,128)(2,1)}), bf16[64,4096]{1,0:T(8,128)(2,1)}) %reduce-scatter.5.cloned.1.call-update) | async-done | bytes 524304 | tf_op jit(solution)/shard_map/reduce_scatter | solution.py:186
  512.9 2.4 convolution_multiply_fusion
  515.4 36.0 %all-reduce.9.cloned.1.call-done = f32[64,4096]{1,0:T(8,128)} async-done(((f32[64,4096]{1,0:T(8,128)}), f32[64,4096]{1,0:T(8,128)}) %all-reduce.9.cloned.1.call-update) | async-done | bytes 1048592 | tf_op jit(solution)/shard_map/psum | solution.py:198
  551.3 2.5 fusion.38
  (74 shorter events, 3.8 us)
Async XLA Ops:
  6.5 54.6 %copy-start = (bf16[1024,1024]{1,0:T(8,128)(2,1)S(1)}, bf16[1024,1024]{1,0:T(8,128)(2,1)}, u32[]{:S(2)}) copy-start(bf16[1024,1024]{1,0:T(8,128)(2,1)} %param.17) | copy-start | bytes 6291460
  6.5 52.3 %copy-start.4 = (bf16[1024,256]{1,0:T(8,128)(2,1)S(1)}, bf16[1024,256]{1,0:T(8,128)(2,1)}, u32[]{:S(2)}) copy-start(bf16[1024,256]{1,0:T(8,128)(2,1)} %param.18) | copy-start | bytes 1572868
  6.5 52.3 %all-gather.4.cloned.1.call-start = ((), (), s32[]{:S(2)}) async-start(), calls=%async_computation.2 | async-start | bytes 2621440 | tf_op jit(solution)/shard_map/all_gather | solution.py:80
  10.0 99.9 %all-reduce.5.cloned.1.call-start = ((), (), s32[]{:S(2)}) async-start(), calls=%async_computation.4 | async-start | bytes 524288 | tf_op jit(solution)/shard_map/psum | solution.py:90
  61.1 64.4 %reduce-scatter.3.cloned.1.call-start = ((), (), s32[]{:S(2)}) async-start(), calls=%async_computation.3 | async-start | bytes 1310720 | tf_op jit(solution)/shard_map/reduce_scatter | solution.py:84
  63.9 0.7 copy-start.11
  63.9 1.0 copy-start.6
  63.9 1.1 copy-start.7
  63.9 21.4 %copy-start.5 = (bf16[1024,256]{1,0:T(8,128)(2,1)S(1)}, bf16[1024,256]{1,0:T(8,128)(2,1)}, u32[]{:S(2)}) copy-start(bf16[1024,256]{1,0:T(8,128)(2,1)} %param.19) | copy-start | bytes 1572868
  63.9 211.2 %all-gather.6.cloned.1.call-start = ((), (), s32[]{:S(2)}) async-start(), calls=%async_computation.5 | async-start | bytes 10485760 | tf_op jit(solution)/shard_map/all_gather | solution.py:150
  64.5 251.1 %all-reduce.7.cloned.1.call-start = ((), (), s32[]{:S(2)}) async-start(), calls=%async_computation.6 | async-start | bytes 2097152 | tf_op jit(solution)/shard_map/psum | solution.py:153
  129.7 151.5 %copy-start.10 = (s32[1,64,2]{1,2,0:T(2,128)S(1)}, s32[1,64,2]{1,2,0:T(2,128)}, u32[]{:S(2)}) copy-start(s32[1,64,2]{1,2,0:T(2,128)} %param.26) | copy-start | bytes 1540
  129.7 185.9 %copy-start.2 = (bf16[64,4096]{1,0:T(8,128)(2,1)S(1)}, bf16[64,4096]{1,0:T(8,128)(2,1)}, u32[]{:S(2)}) copy-start(bf16[64,4096]{1,0:T(8,128)(2,1)} %param.15) | copy-start | bytes 1572868
  281.2 36.0 %copy-start.9 = (f32[4096]{0:T(1024)S(1)}, f32[4096]{0:T(1024)}, u32[]{:S(2)}) copy-start(f32[4096]{0:T(1024)} %param.24) | copy-start | bytes 49156
  281.2 111.4 %all-gather.8.cloned.1.call-start = ((), (), s32[]{:S(2)}) async-start(), calls=%async_computation.7 | async-start | bytes 4718592 | tf_op jit(solution)/shard_map/all_gather | solution.py:179
  315.6 1.6 copy-start.3
  318.7 194.2 %reduce-scatter.5.cloned.1.call-start = ((), (), s32[]{:S(2)}) async-start(), calls=%async_computation.8 | async-start | bytes 4718592 | tf_op jit(solution)/shard_map/reduce_scatter | solution.py:186
  426.5 0.8 copy-start.8
  426.5 124.8 %all-reduce.9.cloned.1.call-start = ((), (), s32[]{:S(2)}) async-start(), calls=%async_computation.9 | async-start | bytes 2097152 | tf_op jit(solution)/shard_map/psum | solution.py:198
  515.3 38.5 %copy-start.1 = (bf16[1024,1024]{1,0:T(8,128)(2,1)S(1)}, bf16[1024,1024]{1,0:T(8,128)(2,1)}, u32[]{:S(2)}) copy-start(bf16[1024,1024]{1,0:T(8,128)(2,1)} %param.17) | copy-start | bytes 6291460
Sparse Core Ops, SparseCore 0:
  10.1 48.6 all-gather.3
  61.2 34.6 all-reduce.4
  98.2 27.1 reduce-scatter.2
  126.8 148.2 all-gather.5
  281.3 34.2 all-reduce.6
  318.8 73.7 all-gather.7
  426.7 86.1 reduce-scatter.4
  515.5 35.8 all-reduce.8
where the time goes:
time: 561 us
  waiting for transfers between devices  438 us (78%)
  matrix products  51.2 us (9%)
  blocking collectives  42.4 us (8%)
  between operations  13.8 us (2%)
  other arithmetic  11.1 us (2%)
    all_gather x1, waiting for transfers between devices, local(): lax.all_gather(out_weight, 'fsdp', axis=1, tiled=True)  145 us
    reduce_scatter x1, waiting for transfers between devices, local(): lax.psum_scatter(jnp.dot(row_block, down_rows, preferred_element_type=jnp...  85.3 us
    all_gather x1, waiting for transfers between devices, local(): piece_rows = lax.all_gather(send_rows, ('dp', 'fsdp'), axis=0, tiled=True)  73.7 us
    all_gather x1, waiting for transfers between devices, local(): everyone = lax.all_gather(normed, 'fsdp', axis=0, tiled=True)  48.7 us
    psum x1, waiting for transfers between devices, local(): mixture = lax.psum(returned * weight_mine[:, None], 'expert')  36 us
    psum x1, waiting for transfers between devices, local(): residual = window.astype(jnp.float32) + lax.psum(head_terms, 'expert')  34 us
    psum x1, blocking collectives, local(): lax.psum((jnp.dot(columns, key_weight, preferred_element_type=jnp.float32...  23.1 us
    dot_general x1, matrix products, local(): jnp.dot(row_block, down_rows, preferred_element_type=jnp.float32)  21.8 us
  transfers between devices with their start and end apart: 8, of which 7 were waited for; matrix products, arithmetic and copies ran while one was open for 2% of the time, Pallas kernels for 0%

commit v1 on v0

--- a/solution.py
+++ b/solution.py
@@ -8,6 +8,24 @@
 epsilon = 1e-05
 rope_base = 1000000.0
 floor_score = -1e30
+
+
+def track_loads_all(vec, dimension_no):
+    val = list(vec.shape[1:])
+    val[dimension_no] *= vec.shape[0]
+    return jnp.moveaxis(vec, 0, dimension_no).reshape(val)
+
+
+def _do_indices(z, bus_axis):
+    devs = lax.axis_size(bus_axis)
+    reached = z[None]
+    for to_i in range(devs.bit_length() - 1):
+        r2 = 1 << to_i
+        next_value = lax.ppermute(reached, bus_axis, tuple(((ix, ix ^ r2) for ix in range(devs))))
+        top = jnp.stack([reached, next_value])
+        arr_out = lax.axis_index(bus_axis) >> to_i & 1
+        reached = jnp.where(arr_out == 0, top, top[::-1]).reshape(-1, *z.shape)
+    return reached
 
 
 def rms_norm(values, scales):
@@ -77,7 +95,7 @@
     first_row = fsdp_place * token_rows
     own_positions = prefix_rows + first_row + jnp.arange(token_rows, dtype=jnp.int32)
     all_positions = prefix_rows + jnp.arange(window_rows, dtype=jnp.int32)
-    everyone = lax.all_gather(normed, "fsdp", axis=0, tiled=True)
+    everyone = track_loads_all(_do_indices(normed, "fsdp"), 0)
     slab_width = query_weight.shape[0]
     columns = lax.dynamic_slice_in_dim(everyone, fsdp_place * slab_width, slab_width, 1)
     row_block = columns

time: 561 us -> 582 us (1.037)
  waiting for transfers between devices: 438 us -> 449 us
    ppermute x0 -> x2, waiting for transfers between devices: none -> 57.3 us  [_do_indices(): lax.ppermute(reached, bus_axis, tuple(((ix, ix ^ r2) for ix in range(devs...]
    all_gather x1 -> x0, waiting for transfers between devices: 48.7 us -> none  [local(): everyone = lax.all_gather(normed, 'fsdp', axis=0, tiled=True)]
    ppermute x0 -> x2, starting transfers between devices: none -> 5.84 us  [_do_indices(): lax.ppermute(reached, bus_axis, tuple(((ix, ix ^ r2) for ix in range(devs...]
  transfers between devices with their start and end apart: 8 -> 9, of which waited for: 7 -> 8; matrix products, arithmetic and copies ran while one was open for 2% -> 2% of each run, Pallas kernels for 0% -> 0%
where the time goes in v1:
time: 582 us
  waiting for transfers between devices  449 us (77%)
  matrix products  50.2 us (9%)
  blocking collectives  43 us (7%)
  other arithmetic  14.6 us (3%)
  between operations  13.8 us (2%)
  starting transfers between devices  6.27 us (1%)
    all_gather x1, waiting for transfers between devices, local(): lax.all_gather(out_weight, 'fsdp', axis=1, tiled=True)  146 us
    reduce_scatter x1, waiting for transfers between devices, local(): lax.psum_scatter(jnp.dot(row_block, down_rows, preferred_element_type=jnp...  85.3 us
    all_gather x1, waiting for transfers between devices, local(): piece_rows = lax.all_gather(send_rows, ('dp', 'fsdp'), axis=0, tiled=True)  73.7 us
    ppermute x2, waiting for transfers between devices, _do_indices(): lax.ppermute(reached, bus_axis, tuple(((ix, ix ^ r2) for ix in range(devs...  57.3 us
    psum x1, waiting for transfers between devices, local(): mixture = lax.psum(returned * weight_mine[:, None], 'expert')  36 us
    psum x1, waiting for transfers between devices, local(): residual = window.astype(jnp.float32) + lax.psum(head_terms, 'expert')  34.1 us
    psum x1, blocking collectives, local(): lax.psum((jnp.dot(columns, key_weight, preferred_element_type=jnp.float32...  24.6 us
    dot_general x1, matrix products, local(): jnp.dot(row_block, down_rows, preferred_element_type=jnp.float32)  21.8 us
  transfers between devices with their start and end apart: 9, of which 8 were waited for; matrix products, arithmetic and copies ran while one was open for 2% of the time, Pallas kernels for 0%

profile of v1, /device:TPU:0, one launch (start us, length us, event | category | flops | bytes accessed | tf_op | source)
XLA Modules:
  0.0 581.6 jit_solution(16294483854638318763)
XLA Ops:
  6.5 1.4 fusion.29
  7.9 1.3 fusion.54
  9.2 3.1 collective-permute-start
  12.3 12.0 %collective-permute-done = bf16[1,64,4096]{2,1,0:T(8,128)(2,1)} collective-permute-done((bf16[1,64,4096]{2,1,0:T(8,128)(2,1)S(1)}, bf16[1,64,4096]{2,1,0:T(8,128)(2,1)}, u32[]{:S(2)}, u32[]{:S(2)}) %collective-permute-start) | collective-permute-done | bytes 524320 | tf_op jit(solution)/shard_map/ppermute | solution.py:24
  24.4 1.1 pad_maximum_fusion.1
  25.5 1.3 fusion.39
  26.8 2.8 collective-permute-start.1
  29.5 45.3 %collective-permute-done.1 = bf16[2,64,4096]{2,1,0:T(8,128)(2,1)} collective-permute-done((bf16[2,64,4096]{2,1,0:T(8,128)(2,1)}, bf16[2,64,4096]{2,1,0:T(8,128)(2,1)}, u32[]{:S(2)}, u32[]{:S(2)}) %collective-permute-start.1) | collective-permute-done | bytes 1048608 | tf_op jit(solution)/shard_map/ppermute | solution.py:24
  74.8 1.4 pad_maximum_fusion
  76.7 1.4 copy-done.4
  78.5 0.8 copy.41
  79.4 2.7 fusion.47
  83.4 4.3 all_gather.15
  87.8 7.0 %all_gather.16 = bf16[1024,256]{0,1:T(8,128)(2,1)S(1)} all-gather(bf16[512,256]{0,1:T(8,128)(2,1)S(1)} %copy.37), channel_id=1, replica_groups=mesh['dp'=2,'fsdp'=4,'expert'=4] {'dp'}, dimensions={0}, use_global_device_ids=true | all-gather | bytes 786432 | tf_op jit(solution)/shard_map/all_gather | solution.py:139
  94.9 7.0 %all_gather.17 = bf16[1024,256]{0,1:T(8,128)(2,1)S(1)} all-gather(bf16[512,256]{0,1:T(8,128)(2,1)S(1)} %copy.39), channel_id=1, replica_groups=mesh['dp'=2,'fsdp'=4,'expert'=4] {'dp'}, dimensions={0}, use_global_device_ids=true | all-gather | bytes 786432 | tf_op jit(solution)/shard_map/all_gather | solution.py:140
  102.8 1.4 fusion.43
  104.1 24.6 %all-reduce.10 = bf16[256,256]{1,0:T(8,128)(2,1)S(1)} all-reduce(f32[256,256]{1,0:T(8,128)S(1)} %fusion.43), channel_id=1, replica_groups=mesh['dp'=2,'fsdp'=4,'expert'=4] {'fsdp'}, use_global_device_ids=true, to_apply=%region_5.6 | all-reduce | flops 65536 | bytes 393216 | tf_op jit(solution)/shard_map/psum | solution.py:108
  128.8 1.2 subtract_convert_fusion
  130.0 15.8 %reduce-scatter.3.cloned.1.call-done = f32[64,1024]{1,0:T(8,128)} async-done(((f32[256,1024]{1,0:T(8,128)}), f32[64,1024]{1,0:T(8,128)}) %reduce-scatter.3.cloned.1.call-update) | async-done | bytes 262160 | tf_op jit(solution)/shard_map/reduce_scatter | solution.py:102
  145.8 1.0 copy.55
  150.1 145.9 %all-gather.3.cloned.1.call-done = bf16[1024,4096]{1,0:T(8,128)(2,1)} async-done(((bf16[1024,1024]{1,0:T(8,128)(2,1)}), bf16[1024,4096]{1,0:T(8,128)(2,1)}) %all-gather.3.cloned.1.call-update) | async-done | bytes 8388624 | tf_op jit(solution)/shard_map/all_gather | solution.py:168
  296.0 6.0 %fusion.84 = f32[64,4096]{1,0:T(8,128)} fusion(bf16[64,1024]{1,0:T(8,128)(2,1)S(1)} %convert_element_type.96, bf16[1024,4096]{1,0:T(8,128)(2,1)} %all-gather.3.cloned.1.call-done), kind=kOutput, calls=%fused_computation.121 | convolution fusion | flops 536870912 | bytes 9568256 | tf_op jit(solution)/shard_map/dot_general | solution.py:166
  302.5 34.1 %all-reduce.7.cloned.1.call-done = f32[64,4096]{1,0:T(8,128)} async-done(((f32[64,4096]{1,0:T(8,128)}), f32[64,4096]{1,0:T(8,128)}) %all-reduce.7.cloned.1.call-update) | async-done | bytes 1048592 | tf_op jit(solution)/shard_map/psum | solution.py:171
  336.6 1.6 multiply_reduce_fusion
  338.3 1.2 convolution_convert_fusion
  339.8 73.7 %all-gather.5.cloned.1.call-done = bf16[512,4096]{1,0:T(8,128)(2,1)} async-done(((bf16[64,4096]{1,0:T(8,128)(2,1)}), bf16[512,4096]{1,0:T(8,128)(2,1)}) %all-gather.5.cloned.1.call-update) | async-done | bytes 4194320 | tf_op jit(solution)/shard_map/all_gather | solution.py:197
  413.5 12.2 %fusion.4 = f32[512,1536]{1,0:T(8,128)} fusion(bf16[512,4096]{1,0:T(8,128)(2,1)} %all-gather.5.cloned.1.call-done, bf16[1,1536,4096]{2,1,0:T(8,128)(2,1)} %param.27), kind=kOutput, calls=%fused_computation.4 | convolution fusion | flops 6442450944 | bytes 19922944 | tf_op jit(solution)/shard_map/dot_general | solution.py:198
  425.7 21.8 %fusion.6 = bf16[512,4096]{1,0:T(8,128)(2,1)} fusion(bf16[1,1536,4096]{2,1,0:T(8,128)(2,1)} %param.29, bf16[512,4096]{1,0:T(8,128)(2,1)} %all-gather.5.cloned.1.call-done, bf16[1,1536,4096]{2,1,0:T(8,128)(2,1)} %param.28, f32[512,1536]{1,0:T(8,128)} %fusion.4), kind=kOutput, calls=%fused_computation.6 | convolution fusion | flops 12891717632 | bytes 36700160 | tf_op jit(solution)/shard_map/dot_general | solution.py:205
  448.5 85.3 %reduce-scatter.5.cloned.1.call-done = bf16[64,4096]{1,0:T(8,128)(2,1)} async-done(((bf16[512,4096]{1,0:T(8,128)(2,1)}), bf16[64,4096]{1,0:T(8,128)(2,1)}) %reduce-scatter.5.cloned.1.call-update) | async-done | bytes 524304 | tf_op jit(solution)/shard_map/reduce_scatter | solution.py:204
  533.8 2.4 convolution_multiply_fusion
  536.3 36.0 %all-reduce.9.cloned.1.call-done = f32[64,4096]{1,0:T(8,128)} async-done(((f32[64,4096]{1,0:T(8,128)}), f32[64,4096]{1,0:T(8,128)}) %all-reduce.9.cloned.1.call-update) | async-done | bytes 1048592 | tf_op jit(solution)/shard_map/psum | solution.py:216
  572.3 2.5 fusion.40
  (81 shorter events, 8.2 us)
Async XLA Ops:
  6.5 72.9 %copy-start = (bf16[1024,1024]{1,0:T(8,128)(2,1)S(1)}, bf16[1024,1024]{1,0:T(8,128)(2,1)}, u32[]{:S(2)}) copy-start(bf16[1024,1024]{1,0:T(8,128)(2,1)} %param.17) | copy-start | bytes 6291460
  6.5 122.2 %all-reduce.5.cloned.1.call-start = ((), (), s32[]{:S(2)}) async-start(), calls=%async_computation.3 | async-start | bytes 524288 | tf_op jit(solution)/shard_map/psum | solution.py:108
  9.2 15.1 %collective-permute-start = (bf16[1,64,4096]{2,1,0:T(8,128)(2,1)S(1)}, bf16[1,64,4096]{2,1,0:T(8,128)(2,1)}, u32[]{:S(2)}, u32[]{:S(2)}) collective-permute-start(bf16[1,64,4096]{2,1,0:T(8,128)(2,1)S(1)} %get-tuple-element.11), channel_id=1, source_target_pairs={{0,4},{4,0},{8,12},{12,8},{1,5},{5,1},{9,13},{13,9},{2,6},{6,2},{1... | collective-permute-start | bytes 1572872 | tf_op jit(solution)/shard_map/ppermute | solution.py:24
  26.8 48.0 %collective-permute-start.1 = (bf16[2,64,4096]{2,1,0:T(8,128)(2,1)}, bf16[2,64,4096]{2,1,0:T(8,128)(2,1)}, u32[]{:S(2)}, u32[]{:S(2)}) collective-permute-start(bf16[2,64,4096]{2,1,0:T(8,128)(2,1)} %get-tuple-element.9), channel_id=1, source_target_pairs={{0,8},{4,12},{8,0},{12,4},{1,9},{5,13},{9,1},{13,5},{2,10},{6,14},... | collective-permute-start | bytes 3145736 | tf_op jit(solution)/shard_map/ppermute | solution.py:24
  76.2 1.9 copy-start.5
  76.7 1.4 copy-start.4
  79.3 66.4 %reduce-scatter.3.cloned.1.call-start = ((), (), s32[]{:S(2)}) async-start(), calls=%async_computation.2 | async-start | bytes 1310720 | tf_op jit(solution)/shard_map/reduce_scatter | solution.py:102
  82.1 0.8 copy-start.12
  82.1 1.0 copy-start.7
  82.1 1.1 copy-start.8
  82.2 20.6 %copy-start.6 = (bf16[1024,256]{1,0:T(8,128)(2,1)S(1)}, bf16[1024,256]{1,0:T(8,128)(2,1)}, u32[]{:S(2)}) copy-start(bf16[1024,256]{1,0:T(8,128)(2,1)} %param.19) | copy-start | bytes 1572868
  82.2 213.9 %all-gather.3.cloned.1.call-start = ((), (), s32[]{:S(2)}) async-start(), calls=%async_computation.4 | async-start | bytes 10485760 | tf_op jit(solution)/shard_map/all_gather | solution.py:168
  82.9 253.6 %all-reduce.7.cloned.1.call-start = ((), (), s32[]{:S(2)}) async-start(), calls=%async_computation.5 | async-start | bytes 2097152 | tf_op jit(solution)/shard_map/psum | solution.py:171
  150.1 152.0 %copy-start.11 = (s32[1,64,2]{1,2,0:T(2,128)S(1)}, s32[1,64,2]{1,2,0:T(2,128)}, u32[]{:S(2)}) copy-start(s32[1,64,2]{1,2,0:T(2,128)} %param.26) | copy-start | bytes 1540
  150.1 186.4 %copy-start.2 = (bf16[64,4096]{1,0:T(8,128)(2,1)S(1)}, bf16[64,4096]{1,0:T(8,128)(2,1)}, u32[]{:S(2)}) copy-start(bf16[64,4096]{1,0:T(8,128)(2,1)} %param.15) | copy-start | bytes 1572868
  302.1 36.1 %copy-start.10 = (f32[4096]{0:T(1024)S(1)}, f32[4096]{0:T(1024)}, u32[]{:S(2)}) copy-start(f32[4096]{0:T(1024)} %param.24) | copy-start | bytes 49156
  302.1 111.4 %all-gather.5.cloned.1.call-start = ((), (), s32[]{:S(2)}) async-start(), calls=%async_computation.6 | async-start | bytes 4718592 | tf_op jit(solution)/shard_map/all_gather | solution.py:197
  336.6 1.6 copy-start.3
  339.6 194.2 %reduce-scatter.5.cloned.1.call-start = ((), (), s32[]{:S(2)}) async-start(), calls=%async_computation.7 | async-start | bytes 4718592 | tf_op jit(solution)/shard_map/reduce_scatter | solution.py:204
  447.5 0.8 copy-start.9
  447.5 124.8 %all-reduce.9.cloned.1.call-start = ((), (), s32[]{:S(2)}) async-start(), calls=%async_computation.8 | async-start | bytes 2097152 | tf_op jit(solution)/shard_map/psum | solution.py:216
  536.2 38.5 %copy-start.1 = (bf16[1024,1024]{1,0:T(8,128)(2,1)S(1)}, bf16[1024,1024]{1,0:T(8,128)(2,1)}, u32[]{:S(2)}) copy-start(bf16[1024,1024]{1,0:T(8,128)(2,1)} %param.17) | copy-start | bytes 6291460
Sparse Core Ops, SparseCore 0:
  79.5 36.9 all-reduce.4
  118.9 26.8 reduce-scatter.2
  147.4 148.6 all-gather.2
  302.2 34.2 all-reduce.6
  339.7 73.7 all-gather.4
  447.6 86.1 reduce-scatter.4
  536.4 35.8 all-reduce.8
